TPU v7x, 32 devices: a whole 2x2x4 slice. The times are simulated.
32 devices in a mesh: slab: 8 (over z, x), tile: 4 (over y, core).
Axes of the slice: x: 2, y: 2, z: 4, core: 2. Of those that a mesh axis runs over, the one named last changes fastest.
Arguments:
- splat_centers_pixel: float32 [8, 2, 2, 1024], P('slab', None, None, 'tile'), may hold values from 0 to 32
- splat_scale: float32 [8, 2, 2, 1024], P('slab', None, None, 'tile'), may hold values from 1 to 6
- splat_angle: float32 [8, 2, 1024], P('slab', None, 'tile'), may hold values from -3.140625 to 3.140625
- splat_opacity: float32 [8, 1024], P('slab', 'tile'), may hold values from 0.002 to 0.08
- splat_color: float32 [8, 3, 1024], P('slab', None, 'tile'), may hold values from 0 to 1
- depth_rank: int32 [8, 2, 1024], P('slab', None, 'tile'), may hold values from 0 to 1023, each once within a row
- dest_tile: int32 [8, 2, 1024, 1], P('slab', None, 'tile'), may hold values from 0 to 3; in each aligned block of 256 rows (0 to 255, 256 to 511, ..., all dimensions but the last counted through in order) at most 128 rows name the same one
- slab_order: int32 [2, 8], replicated, may hold values from 0 to 7, each once within a row
Outputs:
- image: float32 [4, 4, 4096], P(None, 'tile', 'slab')
Inputs may be any that keep to these rules, and one draw needn't show every extreme that they name: `dest_tile`: within each aligned block of 256 rows of a slab and view (the rows of one device), no region is named by more than 128 rows; some region is named by exactly 128 rows in some blocks. `depth_rank`: for each slab and view, every number of 0 to 1023 appears once. `slab_order`: for each view, every slab number appears once.
All inputs are finite; a program needn't handle non-finite values.
Results may differ from a plain program's by a relative error of at most 0.0003.
Values sent between devices are 32-bit elements; how exact they have to be, the bound alone decides.
No kernel may reach another device: no remote copies, remote signals or barrier semaphores. Data moves between devices by JAX's collectives and lax.ppermute only.
A program may use at most 64 MiB of HBM per device.

v0:
```python
from functools import partial
import math

import jax
import jax.numpy as jnp
from jax import lax
from jax.experimental import pallas as pl
from jax.experimental.pallas import tpu as pltpu
from jax.sharding import PartitionSpec as P

PW = 64
PH = 32
NF = 10
HALF_LOG2E = 0.5 * math.log2(math.e)
X_MID = 16.0
LANES = 128
COLOR_AT = 32

f32 = jnp.float32
bf16 = jnp.bfloat16
NT = (((1,), (1,)), ((), ()))


def pieces(x, count):
    out = []
    for _ in range(count):
        part = x.astype(bf16)
        out.append(part)
        x = x - part.astype(f32)
    return out


def sender_kernel(views, tiles, copies, direct, centers, scale, angle, opacity, color, rank, dest, out, feat):
    rows = centers.shape[3]
    cap = 2 * rows // tiles
    slots = tiles * cap
    hot_rows = -(-tiles // 16) * 16

    theta = angle[0]
    cosine = jnp.cos(theta)
    sine = jnp.sin(theta)
    feat[...] = jnp.zeros_like(feat)
    before = lax.broadcasted_iota(jnp.int32, (rows, rows), 0) < lax.broadcasted_iota(jnp.int32, (rows, rows), 1)
    before = jnp.where(before, 1.0, 0.0).astype(bf16)
    tile_id = lax.broadcasted_iota(jnp.int32, (hot_rows, rows), 0)
    slot_id = lax.broadcasted_iota(jnp.int32, (slots, rows), 0)
    for v in range(views):
        s1 = scale[0, v, 0:1]
        s2 = scale[0, v, 1:2]
        i1 = 1.0 / (s1 * s1)
        i2 = 1.0 / (s2 * s2)
        c = cosine[v : v + 1]
        s = sine[v : v + 1]
        feat[v, 0:1] = centers[0, v, 0:1]
        feat[v, 1:2] = centers[0, v, 1:2]
        feat[v, 2:3] = c * c * i1 + s * s * i2
        feat[v, 3:4] = c * s * (i1 - i2)
        feat[v, 4:5] = s * s * i1 + c * c * i2
        feat[v, 5:6] = opacity[0:1]
        feat[v, 6:9] = color[0]
        feat[v, 9:10] = rank[0, v : v + 1].astype(f32)

        target = dest[v : v + 1]
        hot = jnp.where(tile_id == target, 1.0, 0.0)
        earlier = jnp.dot(hot.astype(bf16), before, preferred_element_type=f32)
        place = jnp.sum(hot * earlier, axis=0, keepdims=True).astype(jnp.int32)
        slot = target * cap + place
        pick = jnp.where(slot_id == slot, 1.0, 0.0).astype(bf16)
        stack = jnp.concatenate(pieces(feat[v], 3), axis=0)
        moved = lax.dot_general(stack, pick, NT, preferred_element_type=f32)
        moved = moved[0:16] + moved[16:32] + moved[32:48]
        if direct:
            for t in range(tiles):
                for f in range(NF):
                    row = moved[f : f + 1, t * cap : (t + 1) * cap]
                    for q in range(copies):
                        out[(v * copies + q) * tiles + t, :, f * cap : (f + 1) * cap] = row
        else:
            out[v] = moved[0:NF]


def receiver_kernel(slabs, tiles, views, direct, order, recv, out, feat, coef, sorted_rows, sorted_color, basis):
    entries = feat.shape[2]
    cap = entries // tiles
    columns = out.shape[2]
    blocks = columns // LANES
    pixels = PW * PH
    groups = slabs // 8

    me = lax.axis_index("slab")
    first = me * columns
    view = first // pixels
    y_first = (first - view * pixels) // PW
    half_rows = columns // PW // 2
    y_mid = (y_first + half_rows).astype(f32)

    if direct:
        for f in range(NF):
            for t in range(tiles):
                for k in range(slabs):
                    feat[f, k : k + 1, t * cap : (t + 1) * cap] = recv[k * tiles + t, :, f * cap : (f + 1) * cap]
    else:
        feat[...] = recv[...]

    x = feat[0] - X_MID
    y = feat[1] - y_mid
    a = feat[2]
    b = feat[3]
    c = feat[4]
    o = feat[5]
    h = -HALF_LOG2E
    real = o > 0.0
    ax_by = a * x + b * y
    bx_cy = b * x + c * y
    constant = h * (x * ax_by + y * bx_cy) + jnp.where(real, jnp.log2(jnp.where(real, o, 1.0)), -300.0)
    quad = [h * a, (2.0 * h) * b, h * c]
    lin = [(-2.0 * h) * ax_by, (-2.0 * h) * bx_cy, constant]
    coef[...] = jnp.zeros_like(coef)
    at = 0
    for one in quad:
        parts = [p.astype(f32) for p in pieces(one, 3)]
        for p in parts + parts:
            coef[:, at] = p
            at += 1
    for one in lin:
        for p in pieces(one, 3):
            coef[:, at] = p.astype(f32)
            at += 1
    for i in range(3):
        hi, lo = pieces(feat[6 + i], 2)
        coef[:, COLOR_AT + i] = hi.astype(f32)
        coef[:, LANES + COLOR_AT + i] = lo.astype(f32)

    lane = lax.broadcasted_iota(jnp.int32, (1, columns), 1)
    row = lane // PW
    u = (lane - row * PW).astype(f32) + (0.5 - X_MID)
    w = (row - half_rows).astype(f32) + 0.5
    basis_rows = []
    for one in (u * u, u * w, w * w):
        hi, lo = pieces(one, 2)
        basis_rows += [hi.astype(f32)] * 3 + [lo.astype(f32)] * 3
    basis_rows += [u] * 3 + [w] * 3 + [jnp.ones_like(u)] * 3
    basis[...] = jnp.zeros_like(basis)
    for i, one in enumerate(basis_rows):
        basis[i : i + 1] = one
    monomials = basis[...].astype(bf16)

    lane_e = lax.broadcasted_iota(jnp.int32, (slabs, entries), 1).astype(f32)
    ranks = jnp.where(real, feat[9], lane_e + 1048576.0)
    ranks_t = ranks.T
    chunk = 128
    for k in range(slabs):
        mine = ranks[k : k + 1]
        count = jnp.zeros((8, entries), f32)
        for i in range(entries // 8):
            other = ranks_t[i * 8 : (i + 1) * 8, k : k + 1]
            count = count + jnp.where(other < mine, 1.0, 0.0)
        position = jnp.sum(count, axis=0, keepdims=True).astype(jnp.int32)
        table = coef[k].astype(bf16)
        for j in range(entries // chunk):
            want = lax.broadcasted_iota(jnp.int32, (chunk, entries), 0) + j * chunk
            pick = jnp.where(want == position, 1.0, 0.0).astype(bf16)
            got = lax.dot_general(pick, table, NT, preferred_element_type=f32)
            low = got[:, 0:LANES]
            sorted_rows[pl.ds(j * chunk * slabs + k, chunk, stride=slabs), :] = low
            sorted_color[pl.ds(j * chunk * slabs + k, chunk, stride=slabs), :] = low + got[:, LANES:]

    steps = 256 // slabs
    def blend(i, carry):
        keep, shade = carry
        keep = list(keep)
        shade = list(shade)
        base = pl.multiple_of(i * 256, 256)
        lhs = sorted_rows[pl.ds(base, 256), :].astype(bf16)
        expo = jnp.dot(lhs, monomials, preferred_element_type=f32)
        colors = sorted_color[pl.ds(base, 256), :]
        for s in range(steps):
            for g in range(groups):
                r = (s * groups + g) * 8
                cols = [
                    jnp.broadcast_to(colors[r : r + 8, COLOR_AT + n : COLOR_AT + n + 1], (8, LANES)) for n in range(3)
                ]
                for l in range(blocks):
                    n = g * blocks + l
                    alpha = jnp.exp2(expo[r : r + 8, l * LANES : (l + 1) * LANES])
                    weight = alpha * keep[n]
                    keep[n] = keep[n] - weight
                    for m in range(3):
                        shade[n * 3 + m] = shade[n * 3 + m] + weight * cols[m]
        return tuple(keep), tuple(shade)

    ones = jnp.ones((8, LANES), f32)
    zeros = jnp.zeros((8, LANES), f32)
    state = ((ones,) * (groups * blocks), (zeros,) * (groups * blocks * 3))
    keep, shade = lax.fori_loop(0, entries * slabs // 256, blend, state)

    sub = lax.broadcasted_iota(jnp.int32, (8, LANES), 0)
    orders = []
    for g in range(groups):
        mine = jnp.zeros((8, LANES), jnp.int32)
        for r in range(8):
            mine = jnp.where(sub == r, order[view, g * 8 + r], mine)
        orders.append(mine)
    for l in range(blocks):
        prefix = [ones] * groups
        total = jnp.ones((1, LANES), f32)
        for k in range(slabs):
            other = keep[k // 8 * blocks + l][k % 8 : k % 8 + 1]
            total = total * other
            rank_k = order[view, k]
            for g in range(groups):
                prefix[g] = prefix[g] * jnp.where(rank_k < orders[g], other, 1.0)
        for m in range(3):
            value = jnp.zeros((1, LANES), f32)
            for g in range(groups):
                value = value + jnp.sum(prefix[g] * shade[(g * blocks + l) * 3 + m], axis=0, keepdims=True)
            out[m, :, l * LANES : (l + 1) * LANES] = value
        out[3, :, l * LANES : (l + 1) * LANES] = total


def body(slabs, tiles, centers, scale, angle, opacity, color, rank, dest, order):
    views = centers.shape[1]
    rows = centers.shape[3]
    cap = 2 * rows // tiles
    entries = tiles * cap
    columns = views * PW * PH // slabs
    copies = slabs // views
    direct = cap % LANES == 0
    vmem = pl.BlockSpec(memory_space=pltpu.VMEM)
    smem = pl.BlockSpec(memory_space=pltpu.SMEM)

    out_shape = (slabs * tiles, 1, NF * cap) if direct else (views, NF, entries)
    sent = pl.pallas_call(
        partial(sender_kernel, views, tiles, copies, direct),
        out_shape=jax.ShapeDtypeStruct(out_shape, f32),
        in_specs=[vmem] * 7,
        out_specs=vmem,
        scratch_shapes=[pltpu.VMEM((views, 16, rows), f32)],
        name="sender",
    )(centers, scale, angle, opacity, color, rank, dest[0, :, :, 0])
    if not direct:
        sent = sent.reshape(views, 1, NF, tiles, cap).transpose(0, 1, 3, 2, 4)
        sent = jnp.broadcast_to(sent, (views, copies, tiles, NF, cap)).reshape(slabs * tiles, 1, NF * cap)
    got = lax.all_to_all(sent, ("slab", "tile"), split_axis=0, concat_axis=0, tiled=True)
    if not direct:
        got = got.reshape(slabs, tiles, NF, cap).transpose(2, 0, 1, 3).reshape(NF, slabs, entries)
    return pl.pallas_call(
        partial(receiver_kernel, slabs, tiles, views, direct),
        out_shape=jax.ShapeDtypeStruct((4, 1, columns), f32),
        in_specs=[smem, vmem],
        out_specs=vmem,
        scratch_shapes=[
            pltpu.VMEM((NF, slabs, entries), f32),
            pltpu.VMEM((slabs, 2 * LANES, entries), f32),
            pltpu.VMEM((slabs * entries, LANES), f32),
            pltpu.VMEM((slabs * entries, LANES), f32),
            pltpu.VMEM((LANES, columns), f32),
        ],
        name="receiver",
    )(order, got)


def solution(mesh):
    in_specs = (
        P("slab", None, None, "tile"),
        P("slab", None, None, "tile"),
        P("slab", None, "tile"),
        P("slab", "tile"),
        P("slab", None, "tile"),
        P("slab", None, "tile"),
        P("slab", None, "tile", None),
        P(),
    )
    return jax.shard_map(
        partial(body, mesh.shape["slab"], mesh.shape["tile"]),
        mesh=mesh,
        in_specs=in_specs,
        out_specs=P(None, "tile", "slab"),
        check_vma=False,
    )
```

profile of v0, /device:TPU:0, one launch (start us, length us, event | category | flops | bytes accessed | tf_op | source)
XLA Modules:
  0.0 30.7 jit_solution(13874196046912759687)
XLA Ops:
  0.0 0.0 copy-start
  0.0 1.3 %copy.12 = s32[1,2,256,1]{2,1,3,0:T(2,128)} copy(s32[1,2,256,1]{2,3,1,0:T(1,128)} %param.14) | data formatting | bytes 4096
  1.3 0.0 copy-done
  1.3 0.6 %copy.9.color = f32[1,3,256]{2,1,0:T(4,128)} copy(f32[1,3,256]{2,0,1:T(1,128)S(1)} %copy-done) | data formatting | bytes 6144 | tf_op args[4]
  1.9 2.1 %sender.1 = f32[32,1,1280]{2,1,0:T(1,128)} custom-call(f32[1,2,2,256]{3,2,1,0:T(2,128)} %centers.1, f32[1,2,2,256]{3,2,1,0:T(2,128)} %scale.1, f32[1,2,256]{2,1,0:T(2,128)} %angle.1, f32[1,256]{1,0:T(1,128)} %opacity.1, f32[1,3,256]{2,1,0:T(4,128)} %copy.9.color, s32[1,2,256]{2,1,0:T(2,128)} %rank.1, s32[2,256]{1,0:T(2,128)} %bitcast.3), custom_call_target="tpu_custom_call" | custom-call | tf_op jit(solution)/shard_map/sender/pallas_call | solution.py:233
  4.0 16.1 %all_to_all.5.recv = f32[32,1,1280]{2,1,0:T(1,128)} all-to-all(f32[32,1,1280]{2,1,0:T(1,128)} %sender.1), channel_id=1, replica_groups=mesh['slab'=8,'tile'=4] {'slab','tile'}, dimensions={0} | all-to-all | bytes 327680 | tf_op jit(solution)/shard_map/all_to_all | solution.py:244
  20.0 10.7 %receiver.1 = f32[4,1,512]{2,1,0:T(1,128)} custom-call(s32[2,8]{1,0:T(2,128)} %order.1, f32[32,1,1280]{2,1,0:T(1,128)} %all_to_all.5.recv), custom_call_target="tpu_custom_call" | custom-call | tf_op jit(solution)/shard_map/receiver/pallas_call | solution.py:247
Async XLA Ops:
  0.0 1.3 %copy-start = (f32[1,3,256]{2,0,1:T(1,128)S(1)}, f32[1,3,256]{2,0,1:T(1,128)}, u32[]{:S(2)}) copy-start(f32[1,3,256]{2,0,1:T(1,128)} %param.12) | copy-start | bytes 9220
where the time goes:
time: 31 us; the launch traced here: 30.7 us
  blocking collectives  16.1 us (52%)
  Pallas kernels  12.7 us (41%)
  local copies, waits for them, and re-layouts  1.87 us (6%)
    all_to_all x1, blocking collectives, body(): lax.all_to_all(sent, ('slab', 'tile'), split_axis=0, concat_axis=0, tiled...  16.1 us
    pallas_call x1, Pallas kernels, body(): pl.pallas_call(partial(receiver_kernel, slabs, tiles, views, direct), out...  10.7 us
    pallas_call x1, Pallas kernels, body(): pl.pallas_call(partial(sender_kernel, views, tiles, copies, direct), out_...  2.08 us
    unnamed x4, local copies, waits for them, and re-layouts  1.87 us

commit v1 on v0

v1 whole, which is shorter than its diff:
```python
from functools import partial
import math

import jax
import jax.numpy as jnp
from jax import lax
from jax.experimental import pallas as pl
from jax.experimental.pallas import tpu as pltpu
from jax.sharding import PartitionSpec as P

PW = 64
PH = 32
NF = 10
HALF_LOG2E = 0.5 * math.log2(math.e)
X_MID = 16.0
LANES = 128
ROW = 128
NQ = 27
VALID = 27
COLOR_HI = 28
COLOR_LO = 31
TABLE = 48

f32 = jnp.float32
bf16 = jnp.bfloat16
NT = (((1,), (1,)), ((), ()))


def pieces(x, count):
    out = []
    for _ in range(count):
        part = x.astype(bf16)
        out.append(part)
        x = x - part.astype(f32)
    return out


def sender_kernel(views, tiles, copies, direct, centers, scale, angle, opacity, color, rank, dest, out, feat):
    rows = centers.shape[3]
    cap = 2 * rows // tiles
    slots = tiles * cap
    hot_rows = -(-tiles // 16) * 16

    theta = angle[0]
    cosine = jnp.cos(theta)
    sine = jnp.sin(theta)
    feat[...] = jnp.zeros_like(feat)
    before = lax.broadcasted_iota(jnp.int32, (rows, rows), 0) < lax.broadcasted_iota(jnp.int32, (rows, rows), 1)
    before = jnp.where(before, 1.0, 0.0).astype(bf16)
    tile_id = lax.broadcasted_iota(jnp.int32, (hot_rows, rows), 0)
    slot_id = lax.broadcasted_iota(jnp.int32, (slots, rows), 0)
    for v in range(views):
        s1 = scale[0, v, 0:1]
        s2 = scale[0, v, 1:2]
        i1 = 1.0 / (s1 * s1)
        i2 = 1.0 / (s2 * s2)
        c = cosine[v : v + 1]
        s = sine[v : v + 1]
        feat[v, 0:1] = centers[0, v, 0:1]
        feat[v, 1:2] = centers[0, v, 1:2]
        feat[v, 2:3] = c * c * i1 + s * s * i2
        feat[v, 3:4] = c * s * (i1 - i2)
        feat[v, 4:5] = s * s * i1 + c * c * i2
        feat[v, 5:6] = opacity[0:1]
        for i in range(3):
            feat[v, 6 + i : 7 + i] = color[i]
        feat[v, 9:10] = rank[0, v : v + 1].astype(f32)

        target = dest[0, v]
        hot = jnp.where(tile_id == target, 1.0, 0.0)
        earlier = jnp.dot(hot.astype(bf16), before, preferred_element_type=f32)
        place = jnp.sum(hot * earlier, axis=0, keepdims=True).astype(jnp.int32)
        slot = target * cap + place
        pick = jnp.where(slot_id == slot, 1.0, 0.0).astype(bf16)
        stack = jnp.concatenate(pieces(feat[v], 3), axis=0)
        moved = lax.dot_general(stack, pick, NT, preferred_element_type=f32)
        moved = moved[0:16] + moved[16:32] + moved[32:48]
        if direct:
            for t in range(tiles):
                block = moved[0:NF, t * cap : (t + 1) * cap]
                for q in range(copies):
                    out[pl.ds(((v * copies + q) * tiles + t) * NF, NF), :] = block
        else:
            out[v] = moved[0:NF]


def positions(rank, real, slabs, n_ranks):
    entries = rank.shape[1]
    side = 1 << ((n_ranks - 1).bit_length() + 1) // 2
    together = min(slabs, max(1, 256 // side))
    rows = together * side
    high = jnp.floor(rank * (1.0 / side))
    low = rank - high * side
    high = jnp.where(real, high, 2.0 * side)
    digit = lax.broadcasted_iota(jnp.int32, (rows, entries), 0) % side
    digit = digit.astype(f32)
    same = lax.broadcasted_iota(jnp.int32, (rows, rows), 0) // side
    same = same == lax.broadcasted_iota(jnp.int32, (rows, rows), 1) // side

    def spread(x, k):
        return jnp.concatenate([jnp.broadcast_to(x[k + i : k + i + 1], (side, entries)) for i in range(together)], axis=0)

    def mark(condition):
        return jnp.where(condition, 1.0, 0.0).astype(bf16)

    out = []
    for k in range(0, slabs, together):
        hi = spread(high, k)
        lo = spread(low, k)
        is_hi = hi == digit
        left = jnp.concatenate([mark(is_hi), mark(hi < digit)], axis=1)
        right = jnp.concatenate([mark(lo < digit), jnp.ones((rows, entries), bf16)], axis=1)
        front = lax.dot_general(left, right, NT, preferred_element_type=f32)
        front = jnp.concatenate(pieces(jnp.where(same, front, 0.0), 2), axis=1)
        is_lo = mark(lo == digit)
        mine = jnp.dot(front, jnp.concatenate([is_lo, is_lo], axis=0), preferred_element_type=f32)
        mine = jnp.where(is_hi, mine, 0.0)
        for i in range(together):
            out.append(jnp.sum(mine[i * side : (i + 1) * side], axis=0, keepdims=True))
    return jnp.where(real, jnp.concatenate(out, axis=0), -1.0)


def receiver_kernel(
    slabs, tiles, views, direct, n_ranks, order, recv, out, coef, sorted_rows, basis, q0, q1, w0, w1, em0, em1, acc
):
    entries = coef.shape[0] * LANES
    columns = out.shape[2]
    blocks = columns // LANES
    pixels = PW * PH
    groups = slabs // 8
    chunk = q0.shape[0]
    chunks = slabs * entries // chunk
    shades = 3 * slabs

    me = lax.axis_index("slab")
    first = me * columns
    view = first // pixels
    y_first = (first - view * pixels) // PW
    half_rows = columns // PW // 2
    y_mid = (y_first + half_rows).astype(f32)

    def feature(f):
        if direct:
            return jnp.concatenate(
                [recv[pl.ds(t * NF + f, slabs, stride=tiles * NF), :] for t in range(tiles)], axis=1
            )
        return recv[f]

    o = feature(5)
    real = o > 0.0
    place = positions(feature(9), real, slabs, n_ranks)
    x = feature(0) - X_MID
    y = feature(1) - y_mid
    a = feature(2)
    b = feature(3)
    c = feature(4)
    h = -HALF_LOG2E
    ax_by = a * x + b * y
    bx_cy = b * x + c * y
    constant = h * (x * ax_by + y * bx_cy) + jnp.log2(jnp.where(real, o, 1.0))
    table_rows = []
    for one in (h * a, (2.0 * h) * b, h * c):
        parts = [p.astype(f32) for p in pieces(one, 3)]
        table_rows += parts + parts
    for one in ((-2.0 * h) * ax_by, (-2.0 * h) * bx_cy, constant):
        table_rows += [p.astype(f32) for p in pieces(one, 3)]
    table_rows.append(jnp.ones_like(o))
    colors = [[p.astype(f32) for p in pieces(feature(6 + i), 2)] for i in range(3)]
    table_rows += [p[0] for p in colors] + [p[1] for p in colors]
    table_rows += [jnp.zeros_like(o)] * (TABLE - len(table_rows))
    for i, one in enumerate(table_rows):
        for t in range(entries // LANES):
            coef[t, i * slabs : (i + 1) * slabs, :] = one[:, t * LANES : (t + 1) * LANES]

    lane = lax.broadcasted_iota(jnp.int32, (1, columns), 1)
    row = lane // PW
    u = (lane - row * PW).astype(f32) + (0.5 - X_MID)
    w = (row - half_rows).astype(f32) + 0.5
    basis_rows = []
    for one in (u * u, u * w, w * w):
        hi, lo = pieces(one, 2)
        basis_rows += [hi.astype(f32)] * 3 + [lo.astype(f32)] * 3
    basis_rows += [u] * 3 + [w] * 3 + [jnp.ones_like(u)] * 3 + [jnp.full_like(u, 400.0)]
    basis[...] = jnp.zeros_like(basis)
    for i, one in enumerate(basis_rows):
        basis[i : i + 1] = one
    monomials = basis[...].astype(bf16)

    missing = jnp.where(lax.broadcasted_iota(jnp.int32, (1, ROW), 1) == VALID, -1.0, 0.0)
    want = lax.broadcasted_iota(jnp.int32, (256, entries), 0).astype(f32).astype(bf16)
    zero_rows = jnp.zeros((ROW - TABLE, entries), bf16)
    for k in range(slabs):
        table = [coef[t, pl.ds(k, TABLE, stride=slabs), :] for t in range(entries // LANES)]
        table = jnp.concatenate(table, axis=1).astype(bf16)
        table = jnp.concatenate([table, zero_rows], axis=0)
        for j in range(0, entries, 256):
            mine = jnp.broadcast_to((place[k : k + 1] - j).astype(bf16), (256, entries))
            pick = jnp.where(mine == want, jnp.ones_like(mine), jnp.zeros_like(mine))
            got = lax.dot_general(pick, table, NT, preferred_element_type=f32)
            sorted_rows[pl.ds(j * slabs + k, 256, stride=slabs), :] = got + missing

    which = lax.broadcasted_iota(jnp.int32, (2 * shades, ROW), 0)
    which_lane = lax.broadcasted_iota(jnp.int32, (2 * shades, ROW), 1)
    choose = jnp.where(which // slabs + COLOR_HI == which_lane, 1.0, 0.0).astype(bf16)
    own = lax.broadcasted_iota(jnp.int32, (2 * shades, chunk), 0) % slabs
    own = own == lax.broadcasted_iota(jnp.int32, (2 * shades, chunk), 1) % slabs

    def exponents(i, q, em):
        base = pl.multiple_of(jnp.minimum(i, chunks - 1) * chunk, chunk)
        lhs = sorted_rows[pl.ds(base, chunk), :].astype(bf16)
        q[...] = jnp.dot(lhs, monomials, preferred_element_type=f32)
        picked = lax.dot_general(choose, lhs, NT, preferred_element_type=f32)
        picked = jnp.where(own, picked, 0.0).astype(bf16)
        em[:, 0:chunk] = picked
        em[:, chunk:] = picked

    def weights(q, w, keep):
        keep = list(keep)
        for r in range(0, chunk, 16):
            for l in range(blocks):
                both = []
                for half in range(2):
                    at = r + 8 * half
                    n = at // 8 % groups * blocks + l
                    alpha = jnp.exp2(q[at : at + 8, l * LANES : (l + 1) * LANES])
                    one = alpha * keep[n]
                    keep[n] = keep[n] - one
                    both.append(one)
                both = jnp.concatenate(both, axis=0)
                hi = both.astype(bf16)
                w[r : r + 16, l * LANES : (l + 1) * LANES] = hi
                w[chunk + r : chunk + r + 16, l * LANES : (l + 1) * LANES] = (both - hi.astype(f32)).astype(bf16)
        return tuple(keep)

    def shade(em, w):
        acc[...] += jnp.dot(em[...], w[...], preferred_element_type=f32)

    acc[...] = jnp.zeros_like(acc)
    em1[...] = jnp.zeros_like(em1)
    w1[...] = jnp.zeros_like(w1)
    exponents(0, q0, em0)

    def two_chunks(i, keep):
        shade(em1, w1)
        exponents(2 * i + 1, q1, em1)
        keep = weights(q0, w0, keep)
        shade(em0, w0)
        exponents(2 * i + 2, q0, em0)
        return weights(q1, w1, keep)

    ones = jnp.ones((8, LANES), f32)
    keep = lax.fori_loop(0, chunks // 2, two_chunks, (ones,) * (groups * blocks))
    shade(em1, w1)

    sub = lax.broadcasted_iota(jnp.int32, (8, LANES), 0)
    orders = []
    for g in range(groups):
        mine = jnp.zeros((8, LANES), jnp.int32)
        for r in range(8):
            mine = jnp.where(sub == r, order[view, g * 8 + r], mine)
        orders.append(mine)
    for l in range(blocks):
        at = slice(l * LANES, (l + 1) * LANES)
        prefix = [ones] * groups
        total = jnp.ones((1, LANES), f32)
        for k in range(slabs):
            other = keep[k // 8 * blocks + l][k % 8 : k % 8 + 1]
            total = total * other
            rank_k = order[view, k]
            for g in range(groups):
                prefix[g] = prefix[g] * jnp.where(rank_k < orders[g], other, 1.0)
        for m in range(3):
            value = jnp.zeros((1, LANES), f32)
            for g in range(groups):
                r = m * slabs + g * 8
                value = value + jnp.sum(
                    prefix[g] * (acc[r : r + 8, at] + acc[shades + r : shades + r + 8, at]), axis=0, keepdims=True
                )
            out[m, :, at] = value
        out[3, :, at] = total


def body(slabs, tiles, centers, scale, angle, opacity, color, rank, dest, order):
    views = centers.shape[1]
    rows = centers.shape[3]
    cap = 2 * rows // tiles
    entries = tiles * cap
    columns = views * PW * PH // slabs
    copies = slabs // views
    direct = cap % LANES == 0
    vmem = pl.BlockSpec(memory_space=pltpu.VMEM)
    smem = pl.BlockSpec(memory_space=pltpu.SMEM)

    out_shape = (slabs * tiles * NF, cap) if direct else (views, NF, entries)
    sent = pl.pallas_call(
        partial(sender_kernel, views, tiles, copies, direct),
        out_shape=jax.ShapeDtypeStruct(out_shape, f32),
        in_specs=[vmem] * 7,
        out_specs=vmem,
        scratch_shapes=[pltpu.VMEM((views, 16, rows), f32)],
        name="sender",
    )(centers, scale, angle, opacity, color.transpose(1, 0, 2), rank, dest.transpose(0, 1, 3, 2))
    if not direct:
        sent = sent.reshape(views, 1, NF, tiles, cap).transpose(0, 1, 3, 2, 4)
        sent = jnp.broadcast_to(sent, (views, copies, tiles, NF, cap)).reshape(slabs * tiles, 1, NF * cap)
    sent = sent.reshape(slabs * tiles, 1, NF * cap)
    got = lax.all_to_all(sent, ("slab", "tile"), split_axis=0, concat_axis=0, tiled=True)
    if direct:
        got = got.reshape(slabs * tiles * NF, cap)
    else:
        got = got.reshape(slabs, tiles, NF, cap).transpose(2, 0, 1, 3).reshape(NF, slabs, entries)
    chunk = 256
    width = 6 * slabs
    return pl.pallas_call(
        partial(receiver_kernel, slabs, tiles, views, direct, tiles * rows),
        out_shape=jax.ShapeDtypeStruct((4, 1, columns), f32),
        in_specs=[smem, vmem],
        out_specs=vmem,
        scratch_shapes=[
            pltpu.VMEM((entries // LANES, TABLE * slabs, LANES), f32),
            pltpu.VMEM((slabs * entries, ROW), f32),
            pltpu.VMEM((ROW, columns), f32),
            pltpu.VMEM((chunk, columns), f32),
            pltpu.VMEM((chunk, columns), f32),
            pltpu.VMEM((2 * chunk, columns), bf16),
            pltpu.VMEM((2 * chunk, columns), bf16),
            pltpu.VMEM((width, 2 * chunk), bf16),
            pltpu.VMEM((width, 2 * chunk), bf16),
            pltpu.VMEM((width, columns), f32),
        ],
        name="receiver",
    )(order, got)


def solution(mesh):
    in_specs = (
        P("slab", None, None, "tile"),
        P("slab", None, None, "tile"),
        P("slab", None, "tile"),
        P("slab", "tile"),
        P("slab", None, "tile"),
        P("slab", None, "tile"),
        P("slab", None, "tile", None),
        P(),
    )
    return jax.shard_map(
        partial(body, mesh.shape["slab"], mesh.shape["tile"]),
        mesh=mesh,
        in_specs=in_specs,
        out_specs=P(None, "tile", "slab"),
        check_vma=False,
    )
```

time: 31 us -> 26.3 us (0.85)
  Pallas kernels: 12.7 us -> 10.1 us
  local copies, waits for them, and re-layouts: 1.87 us -> 0 us
    pallas_call x1, Pallas kernels: 10.7 us -> 8 us  [body(): pl.pallas_call(partial(receiver_kernel, slabs, tiles, views, direct, tile...]
    unnamed x4 -> x0, local copies, waits for them, and re-layouts: 1.87 us -> none
where the time goes in v1:
time: 26.3 us; the launch traced here: 26.1 us
  blocking collectives  16.1 us (61%)
  Pallas kernels  10.1 us (38%)
    all_to_all x1, blocking collectives, body(): lax.all_to_all(sent, ('slab', 'tile'), split_axis=0, concat_axis=0, tiled...  16.1 us
    pallas_call x1, Pallas kernels, body(): pl.pallas_call(partial(receiver_kernel, slabs, tiles, views, direct, tile...  8 us
    pallas_call x1, Pallas kernels, body(): pl.pallas_call(partial(sender_kernel, views, tiles, copies, direct), out_...  2.05 us

profile of v1, /device:TPU:0, one launch (start us, length us, event | category | flops | bytes accessed | tf_op | source)
XLA Modules:
  0.0 26.1 jit_solution(12541270879870524006)
XLA Ops:
  0.0 2.1 %sender.1 = f32[320,128]{1,0:T(8,128)} custom-call(f32[1,2,2,256]{3,2,1,0:T(2,128)} %centers.1, f32[1,2,2,256]{3,2,1,0:T(2,128)} %scale.1, f32[1,2,256]{2,1,0:T(2,128)} %angle.1, f32[1,256]{1,0:T(1,128)} %opacity.1, f32[3,1,256]{2,1,0:T(1,128)} %bitcast.6, s32[1,2,256]{2,1,0:T(2,128)} %rank.1, s32[1,2,1,256]{3,2,1,0:T(1,128)} %bitcast.7), custom_call_target="tpu_custom_call" | custom-call | tf_op jit(solution)/shard_map/sender/pallas_call | solution.py:295
  2.1 16.1 %all_to_all.5 = f32[32,1,1280]{2,1,0:T(1,128)} all-to-all(f32[32,1,1280]{2,1,0:T(1,128)} %bitcast.5), channel_id=1, replica_groups=mesh['slab'=8,'tile'=4] {'slab','tile'}, dimensions={0} | all-to-all | bytes 327680 | tf_op jit(solution)/shard_map/all_to_all | solution.py:307
  18.1 8.0 %receiver.1 = f32[4,1,512]{2,1,0:T(1,128)} custom-call(s32[2,8]{1,0:T(2,128)} %order.1, f32[320,128]{1,0:T(8,128)} %bitcast.4), custom_call_target="tpu_custom_call" | custom-call | tf_op jit(solution)/shard_map/receiver/pallas_call | solution.py:314

commit v2 on v1

--- a/solution.py
+++ b/solution.py
@@ -14,12 +14,10 @@
 HALF_LOG2E = 0.5 * math.log2(math.e)
 X_MID = 16.0
 LANES = 128
-ROW = 128
-NQ = 27
-VALID = 27
-COLOR_HI = 28
-COLOR_LO = 31
-TABLE = 48
+GROUP = 32
+STEPS = 64
+VALID = 24
+COLOR = 25
 
 f32 = jnp.float32
 bf16 = jnp.bfloat16
@@ -84,6 +82,10 @@
             out[v] = moved[0:NF]
 
 
+def mark(condition):
+    return jnp.where(condition, jnp.ones(condition.shape, bf16), jnp.zeros(condition.shape, bf16))
+
+
 def positions(rank, real, slabs, n_ranks):
     entries = rank.shape[1]
     side = 1 << ((n_ranks - 1).bit_length() + 1) // 2
@@ -92,44 +94,38 @@
     high = jnp.floor(rank * (1.0 / side))
     low = rank - high * side
     high = jnp.where(real, high, 2.0 * side)
-    digit = lax.broadcasted_iota(jnp.int32, (rows, entries), 0) % side
-    digit = digit.astype(f32)
+    digit = (lax.broadcasted_iota(jnp.int32, (rows, entries), 0) % side).astype(f32)
+    digit_b = digit.astype(bf16)
     same = lax.broadcasted_iota(jnp.int32, (rows, rows), 0) // side
     same = same == lax.broadcasted_iota(jnp.int32, (rows, rows), 1) // side
 
     def spread(x, k):
         return jnp.concatenate([jnp.broadcast_to(x[k + i : k + i + 1], (side, entries)) for i in range(together)], axis=0)
 
-    def mark(condition):
-        return jnp.where(condition, 1.0, 0.0).astype(bf16)
-
     out = []
     for k in range(0, slabs, together):
-        hi = spread(high, k)
-        lo = spread(low, k)
-        is_hi = hi == digit
-        left = jnp.concatenate([mark(is_hi), mark(hi < digit)], axis=1)
-        right = jnp.concatenate([mark(lo < digit), jnp.ones((rows, entries), bf16)], axis=1)
+        hi = spread(high.astype(bf16), k)
+        lo = spread(low.astype(bf16), k)
+        left = jnp.concatenate([mark(hi == digit_b), mark(hi < digit_b)], axis=1)
+        right = jnp.concatenate([mark(lo < digit_b), jnp.ones((rows, entries), bf16)], axis=1)
         front = lax.dot_general(left, right, NT, preferred_element_type=f32)
         front = jnp.concatenate(pieces(jnp.where(same, front, 0.0), 2), axis=1)
-        is_lo = mark(lo == digit)
+        is_lo = mark(lo == digit_b)
         mine = jnp.dot(front, jnp.concatenate([is_lo, is_lo], axis=0), preferred_element_type=f32)
-        mine = jnp.where(is_hi, mine, 0.0)
+        mine = jnp.where(spread(high, k) == digit, mine, 0.0)
         for i in range(together):
             out.append(jnp.sum(mine[i * side : (i + 1) * side], axis=0, keepdims=True))
     return jnp.where(real, jnp.concatenate(out, axis=0), -1.0)
 
 
-def receiver_kernel(
-    slabs, tiles, views, direct, n_ranks, order, recv, out, coef, sorted_rows, basis, q0, q1, w0, w1, em0, em1, acc
-):
+def receiver_kernel(slabs, tiles, views, direct, n_ranks, order, recv, out, coef, lists, basis, q0, q1, w0, w1, acc):
     entries = coef.shape[0] * LANES
     columns = out.shape[2]
     blocks = columns // LANES
     pixels = PW * PH
     groups = slabs // 8
-    chunk = q0.shape[0]
-    chunks = slabs * entries // chunk
+    chunks = entries // STEPS
+    per_row = LANES // GROUP
     shades = 3 * slabs
 
     me = lax.axis_index("slab")
@@ -159,15 +155,14 @@
     bx_cy = b * x + c * y
     constant = h * (x * ax_by + y * bx_cy) + jnp.log2(jnp.where(real, o, 1.0))
     table_rows = []
-    for one in (h * a, (2.0 * h) * b, h * c):
-        parts = [p.astype(f32) for p in pieces(one, 3)]
-        table_rows += parts + parts
+    for one, count in ((h * a, 2), ((2.0 * h) * b, 2), (h * c, 1)):
+        table_rows += [p.astype(f32) for p in pieces(one, 3)] * count
     for one in ((-2.0 * h) * ax_by, (-2.0 * h) * bx_cy, constant):
         table_rows += [p.astype(f32) for p in pieces(one, 3)]
     table_rows.append(jnp.ones_like(o))
     colors = [[p.astype(f32) for p in pieces(feature(6 + i), 2)] for i in range(3)]
     table_rows += [p[0] for p in colors] + [p[1] for p in colors]
-    table_rows += [jnp.zeros_like(o)] * (TABLE - len(table_rows))
+    table_rows += [jnp.zeros_like(o)] * (GROUP - len(table_rows))
     for i, one in enumerate(table_rows):
         for t in range(entries // LANES):
             coef[t, i * slabs : (i + 1) * slabs, :] = one[:, t * LANES : (t + 1) * LANES]
@@ -177,80 +172,77 @@
     u = (lane - row * PW).astype(f32) + (0.5 - X_MID)
     w = (row - half_rows).astype(f32) + 0.5
     basis_rows = []
-    for one in (u * u, u * w, w * w):
-        hi, lo = pieces(one, 2)
-        basis_rows += [hi.astype(f32)] * 3 + [lo.astype(f32)] * 3
+    for one, count in ((u * u, 2), (u * w, 2), (w * w, 1)):
+        for part in pieces(one, count):
+            basis_rows += [part.astype(f32)] * 3
     basis_rows += [u] * 3 + [w] * 3 + [jnp.ones_like(u)] * 3 + [jnp.full_like(u, 400.0)]
     basis[...] = jnp.zeros_like(basis)
     for i, one in enumerate(basis_rows):
-        basis[i : i + 1] = one
-    monomials = basis[...].astype(bf16)
-
-    missing = jnp.where(lax.broadcasted_iota(jnp.int32, (1, ROW), 1) == VALID, -1.0, 0.0)
-    want = lax.broadcasted_iota(jnp.int32, (256, entries), 0).astype(f32).astype(bf16)
-    zero_rows = jnp.zeros((ROW - TABLE, entries), bf16)
+        basis[LANES - GROUP + i : LANES - GROUP + i + 1] = one
+
+    missing = jnp.where(lax.broadcasted_iota(jnp.int32, (1, chunks * GROUP), 1) % GROUP == VALID, -1.0, 0.0)
+    want = lax.broadcasted_iota(jnp.int32, (STEPS, entries), 0).astype(f32).astype(bf16)
+    place_group = jnp.floor(place * (1.0 / STEPS))
+    place_step = (place - place_group * STEPS).astype(bf16)
+    place_group = place_group.astype(bf16)
     for k in range(slabs):
-        table = [coef[t, pl.ds(k, TABLE, stride=slabs), :] for t in range(entries // LANES)]
+        table = [coef[t, pl.ds(k, GROUP, stride=slabs), :] for t in range(entries // LANES)]
         table = jnp.concatenate(table, axis=1).astype(bf16)
-        table = jnp.concatenate([table, zero_rows], axis=0)
-        for j in range(0, entries, 256):
-            mine = jnp.broadcast_to((place[k : k + 1] - j).astype(bf16), (256, entries))
-            pick = jnp.where(mine == want, jnp.ones_like(mine), jnp.zeros_like(mine))
-            got = lax.dot_general(pick, table, NT, preferred_element_type=f32)
-            sorted_rows[pl.ds(j * slabs + k, 256, stride=slabs), :] = got + missing
-
-    which = lax.broadcasted_iota(jnp.int32, (2 * shades, ROW), 0)
-    which_lane = lax.broadcasted_iota(jnp.int32, (2 * shades, ROW), 1)
-    choose = jnp.where(which // slabs + COLOR_HI == which_lane, 1.0, 0.0).astype(bf16)
-    own = lax.broadcasted_iota(jnp.int32, (2 * shades, chunk), 0) % slabs
-    own = own == lax.broadcasted_iota(jnp.int32, (2 * shades, chunk), 1) % slabs
-
-    def exponents(i, q, em):
-        base = pl.multiple_of(jnp.minimum(i, chunks - 1) * chunk, chunk)
-        lhs = sorted_rows[pl.ds(base, chunk), :].astype(bf16)
-        q[...] = jnp.dot(lhs, monomials, preferred_element_type=f32)
-        picked = lax.dot_general(choose, lhs, NT, preferred_element_type=f32)
-        picked = jnp.where(own, picked, 0.0).astype(bf16)
-        em[:, 0:chunk] = picked
-        em[:, chunk:] = picked
+        group = jnp.broadcast_to(place_group[k : k + 1], (GROUP, entries))
+        spread = [
+            jnp.where(group == jnp.full((GROUP, entries), g, bf16), table, jnp.zeros_like(table)) for g in range(chunks)
+        ]
+        spread = jnp.concatenate(spread, axis=0)
+        pick = mark(jnp.broadcast_to(place_step[k : k + 1], (STEPS, entries)) == want)
+        got = lax.dot_general(pick, spread, NT, preferred_element_type=f32) + missing
+        for t in range(chunks // per_row):
+            lists[t, pl.ds(k, STEPS, stride=slabs), :] = got[:, t * LANES : (t + 1) * LANES]
+    sorted_lists = [lists[t].astype(bf16) for t in range(chunks // per_row)]
+
+    shade_rows = []
+    for t in range(chunks // per_row):
+        r = lax.broadcasted_iota(jnp.int32, (per_row * 8, LANES), 0)
+        choose = lax.broadcasted_iota(jnp.int32, (per_row * 8, LANES), 1) == r // 8 * GROUP + COLOR + r % 8
+        choose = jnp.where(choose & (r % 8 < 6), 1.0, 0.0).astype(bf16)
+        shade_rows.append(lax.dot_general(choose, sorted_lists[t], NT, preferred_element_type=f32))
+    own = lax.broadcasted_iota(jnp.int32, (slabs, STEPS * slabs), 0)
+    own = own == lax.broadcasted_iota(jnp.int32, (slabs, STEPS * slabs), 1) % slabs
+
+    def exponents(g, q):
+        first_row = LANES - GROUP - g % per_row * GROUP
+        monomials = basis[first_row : first_row + LANES].astype(bf16)
+        q[...] = jnp.dot(sorted_lists[g // per_row], monomials, preferred_element_type=f32)
 
     def weights(q, w, keep):
         keep = list(keep)
-        for r in range(0, chunk, 16):
+        for r in range(0, STEPS * slabs, 8):
             for l in range(blocks):
-                both = []
-                for half in range(2):
-                    at = r + 8 * half
-                    n = at // 8 % groups * blocks + l
-                    alpha = jnp.exp2(q[at : at + 8, l * LANES : (l + 1) * LANES])
-                    one = alpha * keep[n]
-                    keep[n] = keep[n] - one
-                    both.append(one)
-                both = jnp.concatenate(both, axis=0)
-                hi = both.astype(bf16)
-                w[r : r + 16, l * LANES : (l + 1) * LANES] = hi
-                w[chunk + r : chunk + r + 16, l * LANES : (l + 1) * LANES] = (both - hi.astype(f32)).astype(bf16)
-        return tuple(keep)
-
-    def shade(em, w):
-        acc[...] += jnp.dot(em[...], w[...], preferred_element_type=f32)
-
-    acc[...] = jnp.zeros_like(acc)
-    em1[...] = jnp.zeros_like(em1)
-    w1[...] = jnp.zeros_like(w1)
-    exponents(0, q0, em0)
-
-    def two_chunks(i, keep):
-        shade(em1, w1)
-        exponents(2 * i + 1, q1, em1)
-        keep = weights(q0, w0, keep)
-        shade(em0, w0)
-        exponents(2 * i + 2, q0, em0)
-        return weights(q1, w1, keep)
+                n = r // 8 % groups * blocks + l
+                one = jnp.exp2(q[r : r + 8, l * LANES : (l + 1) * LANES]) * keep[n]
+                keep[n] = keep[n] - one
+                w[r : r + 8, l * LANES : (l + 1) * LANES] = one
+        return keep
+
+    def shade(g, w):
+        rows = [
+            jnp.where(own, shade_rows[g // per_row][g % per_row * 8 + i : g % per_row * 8 + i + 1], 0.0)
+            for i in range(6)
+        ]
+        rows = jnp.concatenate(rows, axis=0).astype(bf16)
+        hi, lo = pieces(w[...], 2)
+        return jnp.dot(
+            jnp.concatenate([rows, rows], axis=1), jnp.concatenate([hi, lo], axis=0), preferred_element_type=f32
+        )
 
     ones = jnp.ones((8, LANES), f32)
-    keep = lax.fori_loop(0, chunks // 2, two_chunks, (ones,) * (groups * blocks))
-    shade(em1, w1)
+    keep = [ones] * (groups * blocks)
+    exponents(0, q0)
+    for g in range(chunks):
+        if g + 1 < chunks:
+            exponents(g + 1, (q0, q1)[(g + 1) % 2])
+        keep = weights((q0, q1)[g % 2], (w0, w1)[g % 2], keep)
+        part = shade(g, (w0, w1)[g % 2])
+        acc[...] = part if g == 0 else acc[...] + part
 
     sub = lax.broadcasted_iota(jnp.int32, (8, LANES), 0)
     orders = []
@@ -309,24 +301,21 @@
         got = got.reshape(slabs * tiles * NF, cap)
     else:
         got = got.reshape(slabs, tiles, NF, cap).transpose(2, 0, 1, 3).reshape(NF, slabs, entries)
-    chunk = 256
-    width = 6 * slabs
+    lanes = entries // STEPS * GROUP
     return pl.pallas_call(
         partial(receiver_kernel, slabs, tiles, views, direct, tiles * rows),
         out_shape=jax.ShapeDtypeStruct((4, 1, columns), f32),
         in_specs=[smem, vmem],
         out_specs=vmem,
         scratch_shapes=[
-            pltpu.VMEM((entries // LANES, TABLE * slabs, LANES), f32),
-            pltpu.VMEM((slabs * entries, ROW), f32),
-            pltpu.VMEM((ROW, columns), f32),
-            pltpu.VMEM((chunk, columns), f32),
-            pltpu.VMEM((chunk, columns), f32),
-            pltpu.VMEM((2 * chunk, columns), bf16),
-            pltpu.VMEM((2 * chunk, columns), bf16),
-            pltpu.VMEM((width, 2 * chunk), bf16),
-            pltpu.VMEM((width, 2 * chunk), bf16),
-            pltpu.VMEM((width, columns), f32),
+            pltpu.VMEM((entries // LANES, GROUP * slabs, LANES), f32),
+            pltpu.VMEM((lanes // LANES, STEPS * slabs, LANES), f32),
+            pltpu.VMEM((2 * LANES - GROUP, columns), f32),
+            pltpu.VMEM((STEPS * slabs, columns), f32),
+            pltpu.VMEM((STEPS * slabs, columns), f32),
+            pltpu.VMEM((STEPS * slabs, columns), f32),
+            pltpu.VMEM((STEPS * slabs, columns), f32),
+            pltpu.VMEM((6 * slabs, columns), f32),
         ],
         name="receiver",
     )(order, got)

time: 26.3 us -> 24.1 us (0.916)
  Pallas kernels: 10.1 us -> 7.83 us
    pallas_call x1, Pallas kernels: 8 us -> 5.77 us  [body(): pl.pallas_call(partial(receiver_kernel, slabs, tiles, views, direct, tile...]
where the time goes in v2:
time: 24.1 us; the launch traced here: 23.9 us
  blocking collectives  16.1 us (67%)
  Pallas kernels  7.83 us (32%)
    all_to_all x1, blocking collectives, body(): lax.all_to_all(sent, ('slab', 'tile'), split_axis=0, concat_axis=0, tiled...  16.1 us
    pallas_call x1, Pallas kernels, body(): pl.pallas_call(partial(receiver_kernel, slabs, tiles, views, direct, tile...  5.77 us
    pallas_call x1, Pallas kernels, body(): pl.pallas_call(partial(sender_kernel, views, tiles, copies, direct), out_...  2.05 us

profile of v2, /device:TPU:0, one launch (start us, length us, event | category | flops | bytes accessed | tf_op | source)
XLA Modules:
  0.0 23.9 jit_solution(12035397986323062021)
XLA Ops:
  0.0 2.1 %sender.1 = f32[320,128]{1,0:T(8,128)} custom-call(f32[1,2,2,256]{3,2,1,0:T(2,128)} %centers.1, f32[1,2,2,256]{3,2,1,0:T(2,128)} %scale.1, f32[1,2,256]{2,1,0:T(2,128)} %angle.1, f32[1,256]{1,0:T(1,128)} %opacity.1, f32[3,1,256]{2,1,0:T(1,128)} %bitcast.6, s32[1,2,256]{2,1,0:T(2,128)} %rank.1, s32[1,2,1,256]{3,2,1,0:T(1,128)} %bitcast.7), custom_call_target="tpu_custom_call" | custom-call | tf_op jit(solution)/shard_map/sender/pallas_call | solution.py:287
  2.1 16.1 %all_to_all.5 = f32[32,1,1280]{2,1,0:T(1,128)} all-to-all(f32[32,1,1280]{2,1,0:T(1,128)} %bitcast.5), channel_id=1, replica_groups=mesh['slab'=8,'tile'=4] {'slab','tile'}, dimensions={0} | all-to-all | bytes 327680 | tf_op jit(solution)/shard_map/all_to_all | solution.py:299
  18.1 5.8 %receiver.1 = f32[4,1,512]{2,1,0:T(1,128)} custom-call(s32[2,8]{1,0:T(2,128)} %order.1, f32[320,128]{1,0:T(8,128)} %bitcast.4), custom_call_target="tpu_custom_call" | custom-call | tf_op jit(solution)/shard_map/receiver/pallas_call | solution.py:305

commit v3 on v2

--- a/solution.py
+++ b/solution.py
@@ -88,37 +88,35 @@
 
 def positions(rank, real, slabs, n_ranks):
     entries = rank.shape[1]
-    side = 1 << ((n_ranks - 1).bit_length() + 1) // 2
-    together = min(slabs, max(1, 256 // side))
-    rows = together * side
-    high = jnp.floor(rank * (1.0 / side))
-    low = rank - high * side
-    high = jnp.where(real, high, 2.0 * side)
-    digit = (lax.broadcasted_iota(jnp.int32, (rows, entries), 0) % side).astype(f32)
-    digit_b = digit.astype(bf16)
-    same = lax.broadcasted_iota(jnp.int32, (rows, rows), 0) // side
-    same = same == lax.broadcasted_iota(jnp.int32, (rows, rows), 1) // side
-
-    def spread(x, k):
-        return jnp.concatenate([jnp.broadcast_to(x[k + i : k + i + 1], (side, entries)) for i in range(together)], axis=0)
-
+    tall = 16
+    wide = -(-n_ranks // tall)
+    high = jnp.floor(rank * (1.0 / wide))
+    low = (rank - high * wide).astype(bf16)
+    high = jnp.where(real, high, 2.0 * tall)
+    high_b = high.astype(bf16)
+    tall_f = lax.broadcasted_iota(jnp.int32, (tall, entries), 0).astype(f32)
+    tall_b = tall_f.astype(bf16)
+    wide_b = lax.broadcasted_iota(jnp.int32, (wide, entries), 0).astype(f32).astype(bf16)
+    ones = jnp.ones((wide, entries), bf16)
+
+    fronts = []
+    for k in range(slabs):
+        hi = jnp.broadcast_to(high_b[k : k + 1], (tall, entries))
+        lo = jnp.broadcast_to(low[k : k + 1], (wide, entries))
+        left = jnp.concatenate([mark(hi == tall_b), mark(hi < tall_b)], axis=1)
+        right = jnp.concatenate([mark(lo < wide_b), ones], axis=1)
+        front = lax.dot_general(left, right, NT, preferred_element_type=f32)
+        fronts.append(jnp.concatenate(pieces(front, 2), axis=1))
     out = []
-    for k in range(0, slabs, together):
-        hi = spread(high.astype(bf16), k)
-        lo = spread(low.astype(bf16), k)
-        left = jnp.concatenate([mark(hi == digit_b), mark(hi < digit_b)], axis=1)
-        right = jnp.concatenate([mark(lo < digit_b), jnp.ones((rows, entries), bf16)], axis=1)
-        front = lax.dot_general(left, right, NT, preferred_element_type=f32)
-        front = jnp.concatenate(pieces(jnp.where(same, front, 0.0), 2), axis=1)
-        is_lo = mark(lo == digit_b)
-        mine = jnp.dot(front, jnp.concatenate([is_lo, is_lo], axis=0), preferred_element_type=f32)
-        mine = jnp.where(spread(high, k) == digit, mine, 0.0)
-        for i in range(together):
-            out.append(jnp.sum(mine[i * side : (i + 1) * side], axis=0, keepdims=True))
+    for k in range(slabs):
+        is_lo = mark(jnp.broadcast_to(low[k : k + 1], (wide, entries)) == wide_b)
+        mine = jnp.dot(fronts[k], jnp.concatenate([is_lo, is_lo], axis=0), preferred_element_type=f32)
+        mine = jnp.where(high[k : k + 1] == tall_f, mine, 0.0)
+        out.append(jnp.sum(mine, axis=0, keepdims=True))
     return jnp.where(real, jnp.concatenate(out, axis=0), -1.0)
 
 
-def receiver_kernel(slabs, tiles, views, direct, n_ranks, order, recv, out, coef, lists, basis, q0, q1, w0, w1, acc):
+def receiver_kernel(slabs, tiles, views, direct, n_ranks, order_hbm, recv, out, coef, lists, basis, q0, q1, w0, w1, acc, order, order_sem):
     entries = coef.shape[0] * LANES
     columns = out.shape[2]
     blocks = columns // LANES
@@ -128,6 +126,8 @@
     per_row = LANES // GROUP
     shades = 3 * slabs
 
+    fetch = pltpu.make_async_copy(order_hbm, order, order_sem)
+    fetch.start()
     me = lax.axis_index("slab")
     first = me * columns
     view = first // pixels
@@ -244,6 +244,7 @@
         part = shade(g, (w0, w1)[g % 2])
         acc[...] = part if g == 0 else acc[...] + part
 
+    fetch.wait()
     sub = lax.broadcasted_iota(jnp.int32, (8, LANES), 0)
     orders = []
     for g in range(groups):
@@ -281,12 +282,11 @@
     copies = slabs // views
     direct = cap % LANES == 0
     vmem = pl.BlockSpec(memory_space=pltpu.VMEM)
-    smem = pl.BlockSpec(memory_space=pltpu.SMEM)
 
     out_shape = (slabs * tiles * NF, cap) if direct else (views, NF, entries)
     sent = pl.pallas_call(
         partial(sender_kernel, views, tiles, copies, direct),
-        out_shape=jax.ShapeDtypeStruct(out_shape, f32),
+        out_shape=pltpu.VMEM(out_shape, f32),
         in_specs=[vmem] * 7,
         out_specs=vmem,
         scratch_shapes=[pltpu.VMEM((views, 16, rows), f32)],
@@ -305,7 +305,7 @@
     return pl.pallas_call(
         partial(receiver_kernel, slabs, tiles, views, direct, tiles * rows),
         out_shape=jax.ShapeDtypeStruct((4, 1, columns), f32),
-        in_specs=[smem, vmem],
+        in_specs=[pl.BlockSpec(memory_space=pl.ANY), vmem],
         out_specs=vmem,
         scratch_shapes=[
             pltpu.VMEM((entries // LANES, GROUP * slabs, LANES), f32),
@@ -316,9 +316,11 @@
             pltpu.VMEM((STEPS * slabs, columns), f32),
             pltpu.VMEM((STEPS * slabs, columns), f32),
             pltpu.VMEM((6 * slabs, columns), f32),
+            pltpu.SMEM(order.shape, jnp.int32),
+            pltpu.SemaphoreType.DMA,
         ],
         name="receiver",
-    )(order, got)
+    )(order, pltpu.with_memory_space_constraint(got, pltpu.VMEM))
 
 
 def solution(mesh):

time: 24.1 us -> 22.2 us (0.921)
  Pallas kernels: 7.83 us -> 6.21 us
  blocking collectives: 16.1 us -> 15.8 us
    pallas_call x1, Pallas kernels: 5.77 us -> 4.82 us  [body(): pl.pallas_call(partial(receiver_kernel, slabs, tiles, views, direct, tile...]
    pallas_call x1, Pallas kernels: 2.05 us -> 1.4 us  [body(): pl.pallas_call(partial(sender_kernel, views, tiles, copies, direct), out_...]
    all_to_all x1, blocking collectives: 16.1 us -> 15.8 us  [body(): lax.all_to_all(sent, ('slab', 'tile'), split_axis=0, concat_axis=0, tiled...]
where the time goes in v3:
time: 22.2 us; the launch traced here: 22 us
  blocking collectives  15.8 us (71%)
  Pallas kernels  6.21 us (28%)
    all_to_all x1, blocking collectives, body(): lax.all_to_all(sent, ('slab', 'tile'), split_axis=0, concat_axis=0, tiled...  15.8 us
    pallas_call x1, Pallas kernels, body(): pl.pallas_call(partial(receiver_kernel, slabs, tiles, views, direct, tile...  4.82 us
    pallas_call x1, Pallas kernels, body(): pl.pallas_call(partial(sender_kernel, views, tiles, copies, direct), out_...  1.4 us

profile of v3, /device:TPU:0, one launch (start us, length us, event | category | flops | bytes accessed | tf_op | source)
XLA Modules:
  0.0 22.0 jit_solution(9364541856768879752)
XLA Ops:
  0.0 1.4 %sender.1 = f32[320,128]{1,0:T(8,128)S(1)} custom-call(f32[1,2,2,256]{3,2,1,0:T(2,128)} %centers.1, f32[1,2,2,256]{3,2,1,0:T(2,128)} %scale.1, f32[1,2,256]{2,1,0:T(2,128)} %angle.1, f32[1,256]{1,0:T(1,128)} %opacity.1, f32[3,1,256]{2,1,0:T(1,128)} %bitcast.6, s32[1,2,256]{2,1,0:T(2,128)} %rank.1, s32[1,2,1,256]{3,2,1,0:T(1,128)} %bitcast.7), custom_call_target="tpu_custom_call" | custom-call | tf_op jit(solution)/shard_map/sender/pallas_call | solution.py:287
  1.4 15.8 %all_to_all.5 = f32[32,1,1280]{2,1,0:T(1,128)S(1)} all-to-all(f32[32,1,1280]{2,1,0:T(1,128)S(1)} %bitcast.5), channel_id=1, replica_groups=mesh['slab'=8,'tile'=4] {'slab','tile'}, dimensions={0} | all-to-all | bytes 327680 | tf_op jit(solution)/shard_map/all_to_all | solution.py:299
  17.2 4.8 %receiver.1 = f32[4,1,512]{2,1,0:T(1,128)} custom-call(s32[2,8]{1,0:T(2,128)} %order_hbm.1, f32[320,128]{1,0:T(8,128)S(1)} %bitcast.4), custom_call_target="tpu_custom_call" | custom-call | tf_op jit(solution)/shard_map/receiver/pallas_call | solution.py:305

commit v4 on v3

--- a/solution.py
+++ b/solution.py
@@ -15,7 +15,10 @@
 X_MID = 16.0
 LANES = 128
 GROUP = 32
-STEPS = 64
+PART = 16
+AHEAD = 2
+LAG = 2
+STEPS = 128
 VALID = 24
 COLOR = 25
 
@@ -88,7 +91,7 @@
 
 def positions(rank, real, slabs, n_ranks):
     entries = rank.shape[1]
-    tall = 16
+    tall = 32
     wide = -(-n_ranks // tall)
     high = jnp.floor(rank * (1.0 / wide))
     low = (rank - high * wide).astype(bf16)
@@ -116,7 +119,7 @@
     return jnp.where(real, jnp.concatenate(out, axis=0), -1.0)
 
 
-def receiver_kernel(slabs, tiles, views, direct, n_ranks, order_hbm, recv, out, coef, lists, basis, q0, q1, w0, w1, acc, order, order_sem):
+def receiver_kernel(slabs, tiles, views, direct, n_ranks, order_hbm, recv, out, coef, lists, basis, acc, order, order_sem):
     entries = coef.shape[0] * LANES
     columns = out.shape[2]
     blocks = columns // LANES
@@ -205,44 +208,60 @@
         choose = lax.broadcasted_iota(jnp.int32, (per_row * 8, LANES), 1) == r // 8 * GROUP + COLOR + r % 8
         choose = jnp.where(choose & (r % 8 < 6), 1.0, 0.0).astype(bf16)
         shade_rows.append(lax.dot_general(choose, sorted_lists[t], NT, preferred_element_type=f32))
-    own = lax.broadcasted_iota(jnp.int32, (slabs, STEPS * slabs), 0)
-    own = own == lax.broadcasted_iota(jnp.int32, (slabs, STEPS * slabs), 1) % slabs
-
-    def exponents(g, q):
+    own = lax.broadcasted_iota(jnp.int32, (slabs, PART * slabs), 0)
+    own = own == lax.broadcasted_iota(jnp.int32, (slabs, PART * slabs), 1) % slabs
+
+    rows = PART * slabs
+    per_chunk = STEPS // PART
+
+    def exponents(n):
+        g, p = n // per_chunk, n % per_chunk
         first_row = LANES - GROUP - g % per_row * GROUP
         monomials = basis[first_row : first_row + LANES].astype(bf16)
-        q[...] = jnp.dot(sorted_lists[g // per_row], monomials, preferred_element_type=f32)
-
-    def weights(q, w, keep):
-        keep = list(keep)
-        for r in range(0, STEPS * slabs, 8):
+        lhs = sorted_lists[g // per_row][p * rows : (p + 1) * rows]
+        return jnp.dot(lhs, monomials, preferred_element_type=f32)
+
+    def weights(q, keep):
+        highs = []
+        lows = []
+        for r in range(0, rows, 16):
+            hi_row = []
+            lo_row = []
             for l in range(blocks):
-                n = r // 8 % groups * blocks + l
-                one = jnp.exp2(q[r : r + 8, l * LANES : (l + 1) * LANES]) * keep[n]
-                keep[n] = keep[n] - one
-                w[r : r + 8, l * LANES : (l + 1) * LANES] = one
-        return keep
-
-    def shade(g, w):
-        rows = [
-            jnp.where(own, shade_rows[g // per_row][g % per_row * 8 + i : g % per_row * 8 + i + 1], 0.0)
-            for i in range(6)
-        ]
-        rows = jnp.concatenate(rows, axis=0).astype(bf16)
-        hi, lo = pieces(w[...], 2)
-        return jnp.dot(
-            jnp.concatenate([rows, rows], axis=1), jnp.concatenate([hi, lo], axis=0), preferred_element_type=f32
-        )
+                both = []
+                for at in (r, r + 8):
+                    i = at // 8 % groups * blocks + l
+                    one = jnp.exp2(q[at : at + 8, l * LANES : (l + 1) * LANES]) * keep[i]
+                    keep[i] = keep[i] - one
+                    both.append(one)
+                hi, lo = pieces(jnp.concatenate(both, axis=0), 2)
+                hi_row.append(hi)
+                lo_row.append(lo)
+            highs.append(jnp.concatenate(hi_row, axis=1))
+            lows.append(jnp.concatenate(lo_row, axis=1))
+        return jnp.concatenate(highs + lows, axis=0)
+
+    def colours(n):
+        g, p = n // per_chunk, n % per_chunk
+        some = shade_rows[g // per_row][g % per_row * 8 : g % per_row * 8 + 8, p * rows : (p + 1) * rows]
+        some = [jnp.where(own, some[i : i + 1], 0.0) for i in range(6)]
+        some = jnp.concatenate(some, axis=0).astype(bf16)
+        return jnp.concatenate([some, some], axis=1)
 
     ones = jnp.ones((8, LANES), f32)
     keep = [ones] * (groups * blocks)
-    exponents(0, q0)
-    for g in range(chunks):
-        if g + 1 < chunks:
-            exponents(g + 1, (q0, q1)[(g + 1) % 2])
-        keep = weights((q0, q1)[g % 2], (w0, w1)[g % 2], keep)
-        part = shade(g, (w0, w1)[g % 2])
-        acc[...] = part if g == 0 else acc[...] + part
+    total = jnp.zeros((6 * slabs, columns), f32)
+    parts = chunks * per_chunk
+    ahead = [exponents(n) for n in range(AHEAD)]
+    behind = []
+    for n in range(parts + LAG):
+        if n >= LAG:
+            total = total + jnp.dot(colours(n - LAG), behind.pop(0), preferred_element_type=f32)
+        if n + AHEAD < parts:
+            ahead.append(exponents(n + AHEAD))
+        if n < parts:
+            behind.append(weights(ahead.pop(0), keep))
+    acc[...] = total
 
     fetch.wait()
     sub = lax.broadcasted_iota(jnp.int32, (8, LANES), 0)
@@ -311,10 +330,6 @@
             pltpu.VMEM((entries // LANES, GROUP * slabs, LANES), f32),
             pltpu.VMEM((lanes // LANES, STEPS * slabs, LANES), f32),
             pltpu.VMEM((2 * LANES - GROUP, columns), f32),
-            pltpu.VMEM((STEPS * slabs, columns), f32),
-            pltpu.VMEM((STEPS * slabs, columns), f32),
-            pltpu.VMEM((STEPS * slabs, columns), f32),
-            pltpu.VMEM((STEPS * slabs, columns), f32),
             pltpu.VMEM((6 * slabs, columns), f32),
             pltpu.SMEM(order.shape, jnp.int32),
             pltpu.SemaphoreType.DMA,

time: 22.2 us -> 21.1 us (0.950)
  Pallas kernels: 6.21 us -> 5.17 us
    pallas_call x1, Pallas kernels: 4.82 us -> 3.78 us  [body(): pl.pallas_call(partial(receiver_kernel, slabs, tiles, views, direct, tile...]
where the time goes in v4:
time: 21.1 us; the launch traced here: 20.9 us
  blocking collectives  15.8 us (75%)
  Pallas kernels  5.17 us (25%)
    all_to_all x1, blocking collectives, body(): lax.all_to_all(sent, ('slab', 'tile'), split_axis=0, concat_axis=0, tiled...  15.8 us
    pallas_call x1, Pallas kernels, body(): pl.pallas_call(partial(receiver_kernel, slabs, tiles, views, direct, tile...  3.78 us
    pallas_call x1, Pallas kernels, body(): pl.pallas_call(partial(sender_kernel, views, tiles, copies, direct), out_...  1.4 us

profile of v4, /device:TPU:0, one launch (start us, length us, event | category | flops | bytes accessed | tf_op | source)
XLA Modules:
  0.0 20.9 jit_solution(119816680208446703)
XLA Ops:
  0.0 1.4 %sender.1 = f32[320,128]{1,0:T(8,128)S(1)} custom-call(f32[1,2,2,256]{3,2,1,0:T(2,128)} %centers.1, f32[1,2,2,256]{3,2,1,0:T(2,128)} %scale.1, f32[1,2,256]{2,1,0:T(2,128)} %angle.1, f32[1,256]{1,0:T(1,128)} %opacity.1, f32[3,1,256]{2,1,0:T(1,128)} %bitcast.6, s32[1,2,256]{2,1,0:T(2,128)} %rank.1, s32[1,2,1,256]{3,2,1,0:T(1,128)} %bitcast.7), custom_call_target="tpu_custom_call" | custom-call | tf_op jit(solution)/shard_map/sender/pallas_call | solution.py:306
  1.4 15.8 %all_to_all.5 = f32[32,1,1280]{2,1,0:T(1,128)S(1)} all-to-all(f32[32,1,1280]{2,1,0:T(1,128)S(1)} %bitcast.5), channel_id=1, replica_groups=mesh['slab'=8,'tile'=4] {'slab','tile'}, dimensions={0} | all-to-all | bytes 327680 | tf_op jit(solution)/shard_map/all_to_all | solution.py:318
  17.2 3.8 %receiver.1 = f32[4,1,512]{2,1,0:T(1,128)} custom-call(s32[2,8]{1,0:T(2,128)} %order_hbm.1, f32[320,128]{1,0:T(8,128)S(1)} %bitcast.4), custom_call_target="tpu_custom_call" | custom-call | tf_op jit(solution)/shard_map/receiver/pallas_call | solution.py:324

commit v5 on v4

--- a/solution.py
+++ b/solution.py
@@ -18,6 +18,7 @@
 PART = 16
 AHEAD = 2
 LAG = 2
+STOPS = (5, 6, 7, 8, 9, 16)
 STEPS = 128
 VALID = 24
 COLOR = 25
@@ -119,7 +120,7 @@
     return jnp.where(real, jnp.concatenate(out, axis=0), -1.0)
 
 
-def receiver_kernel(slabs, tiles, views, direct, n_ranks, order_hbm, recv, out, coef, lists, basis, acc, order, order_sem):
+def receiver_kernel(slabs, tiles, views, direct, n_ranks, order_hbm, recv, out, coef, lists, basis, acc, kept, order, order_sem):
     entries = coef.shape[0] * LANES
     columns = out.shape[2]
     blocks = columns // LANES
@@ -147,6 +148,7 @@
 
     o = feature(5)
     real = o > 0.0
+    longest = jnp.max(jnp.sum(jnp.where(real, 1.0, 0.0), axis=1))
     place = positions(feature(9), real, slabs, n_ranks)
     x = feature(0) - X_MID
     y = feature(1) - y_mid
@@ -200,21 +202,17 @@
         got = lax.dot_general(pick, spread, NT, preferred_element_type=f32) + missing
         for t in range(chunks // per_row):
             lists[t, pl.ds(k, STEPS, stride=slabs), :] = got[:, t * LANES : (t + 1) * LANES]
-    sorted_lists = [lists[t].astype(bf16) for t in range(chunks // per_row)]
-
-    shade_rows = []
-    for t in range(chunks // per_row):
-        r = lax.broadcasted_iota(jnp.int32, (per_row * 8, LANES), 0)
-        choose = lax.broadcasted_iota(jnp.int32, (per_row * 8, LANES), 1) == r // 8 * GROUP + COLOR + r % 8
-        choose = jnp.where(choose & (r % 8 < 6), 1.0, 0.0).astype(bf16)
-        shade_rows.append(lax.dot_general(choose, sorted_lists[t], NT, preferred_element_type=f32))
+
     own = lax.broadcasted_iota(jnp.int32, (slabs, PART * slabs), 0)
     own = own == lax.broadcasted_iota(jnp.int32, (slabs, PART * slabs), 1) % slabs
 
     rows = PART * slabs
     per_chunk = STEPS // PART
 
-    def exponents(n):
+    parts = chunks * per_chunk
+    ones = jnp.ones((8, LANES), f32)
+
+    def exponents(sorted_lists, n):
         g, p = n // per_chunk, n % per_chunk
         first_row = LANES - GROUP - g % per_row * GROUP
         monomials = basis[first_row : first_row + LANES].astype(bf16)
@@ -241,27 +239,44 @@
             lows.append(jnp.concatenate(lo_row, axis=1))
         return jnp.concatenate(highs + lows, axis=0)
 
-    def colours(n):
+    def colours(shade_rows, n):
         g, p = n // per_chunk, n % per_chunk
         some = shade_rows[g // per_row][g % per_row * 8 : g % per_row * 8 + 8, p * rows : (p + 1) * rows]
         some = [jnp.where(own, some[i : i + 1], 0.0) for i in range(6)]
         some = jnp.concatenate(some, axis=0).astype(bf16)
         return jnp.concatenate([some, some], axis=1)
 
-    ones = jnp.ones((8, LANES), f32)
-    keep = [ones] * (groups * blocks)
-    total = jnp.zeros((6 * slabs, columns), f32)
-    parts = chunks * per_chunk
-    ahead = [exponents(n) for n in range(AHEAD)]
-    behind = []
-    for n in range(parts + LAG):
-        if n >= LAG:
-            total = total + jnp.dot(colours(n - LAG), behind.pop(0), preferred_element_type=f32)
-        if n + AHEAD < parts:
-            ahead.append(exponents(n + AHEAD))
-        if n < parts:
-            behind.append(weights(ahead.pop(0), keep))
-    acc[...] = total
+    def blend(parts):
+        sorted_lists = [lists[t].astype(bf16) for t in range(chunks // per_row)]
+        keep = [ones] * (groups * blocks)
+        total = jnp.zeros((6 * slabs, columns), f32)
+        ahead = [exponents(sorted_lists, n) for n in range(AHEAD)]
+        shade_rows = []
+        for t in range(chunks // per_row):
+            r = lax.broadcasted_iota(jnp.int32, (per_row * 8, LANES), 0)
+            choose = lax.broadcasted_iota(jnp.int32, (per_row * 8, LANES), 1) == r // 8 * GROUP + COLOR + r % 8
+            choose = jnp.where(choose & (r % 8 < 6), 1.0, 0.0).astype(bf16)
+            shade_rows.append(lax.dot_general(choose, sorted_lists[t], NT, preferred_element_type=f32))
+
+        behind = []
+        for n in range(parts + LAG):
+            if n >= LAG:
+                total = total + jnp.dot(colours(shade_rows, n - LAG), behind.pop(0), preferred_element_type=f32)
+            if n + AHEAD < parts:
+                ahead.append(exponents(sorted_lists, n + AHEAD))
+            if n < parts:
+                behind.append(weights(ahead.pop(0), keep))
+        acc[...] = total
+        for i, one in enumerate(keep):
+            kept[i] = one
+
+    floor = -1
+    for sixteenths in STOPS:
+        most = parts * sixteenths // 16
+        fits = (longest > floor * PART) & (longest <= most * PART)
+        pl.when(fits)(partial(blend, most))
+        floor = most
+    keep = [kept[i] for i in range(groups * blocks)]
 
     fetch.wait()
     sub = lax.broadcasted_iota(jnp.int32, (8, LANES), 0)
@@ -331,6 +346,7 @@
             pltpu.VMEM((lanes // LANES, STEPS * slabs, LANES), f32),
             pltpu.VMEM((2 * LANES - GROUP, columns), f32),
             pltpu.VMEM((6 * slabs, columns), f32),
+            pltpu.VMEM((slabs // 8 * columns // LANES, 8, LANES), f32),
             pltpu.SMEM(order.shape, jnp.int32),
             pltpu.SemaphoreType.DMA,
         ],

time: 21.1 us -> 21.1 us (level)
  the two profiles are of different devices: /device:TPU:0 before, /device:TPU:1 now
where the time goes in v5:
time: 21.1 us; the launch traced here: 20.9 us
  blocking collectives  15.6 us (74%)
  Pallas kernels  5.31 us (25%)
    all_to_all x1, blocking collectives, body(): lax.all_to_all(sent, ('slab', 'tile'), split_axis=0, concat_axis=0, tiled...  15.6 us
    pallas_call x1, Pallas kernels, body(): pl.pallas_call(partial(receiver_kernel, slabs, tiles, views, direct, tile...  3.91 us
    pallas_call x1, Pallas kernels, body(): pl.pallas_call(partial(sender_kernel, views, tiles, copies, direct), out_...  1.4 us

profile of v5, /device:TPU:1, one launch (start us, length us, event | category | flops | bytes accessed | tf_op | source)
XLA Modules:
  0.0 20.9 jit_solution(2547227766603521314)
XLA Ops:
  0.0 1.4 %sender.1 = f32[320,128]{1,0:T(8,128)S(1)} custom-call(f32[1,2,2,256]{3,2,1,0:T(2,128)} %centers.1, f32[1,2,2,256]{3,2,1,0:T(2,128)} %scale.1, f32[1,2,256]{2,1,0:T(2,128)} %angle.1, f32[1,256]{1,0:T(1,128)} %opacity.1, f32[3,1,256]{2,1,0:T(1,128)} %bitcast.6, s32[1,2,256]{2,1,0:T(2,128)} %rank.1, s32[1,2,1,256]{3,2,1,0:T(1,128)} %bitcast.7), custom_call_target="tpu_custom_call" | custom-call | tf_op jit(solution)/shard_map/sender/pallas_call | solution.py:321
  1.4 15.6 %all_to_all.5 = f32[32,1,1280]{2,1,0:T(1,128)S(1)} all-to-all(f32[32,1,1280]{2,1,0:T(1,128)S(1)} %bitcast.5), channel_id=1, replica_groups=mesh['slab'=8,'tile'=4] {'slab','tile'}, dimensions={0} | all-to-all | bytes 327680 | tf_op jit(solution)/shard_map/all_to_all | solution.py:333
  17.0 3.9 %receiver.1 = f32[4,1,512]{2,1,0:T(1,128)} custom-call(s32[2,8]{1,0:T(2,128)} %order_hbm.1, f32[320,128]{1,0:T(8,128)S(1)} %bitcast.4), custom_call_target="tpu_custom_call" | custom-call | tf_op jit(solution)/shard_map/receiver/pallas_call | solution.py:339

commit v6 on v5

--- a/solution.py
+++ b/solution.py
@@ -37,6 +37,10 @@
     return out
 
 
+def mark(condition):
+    return jnp.where(condition, jnp.ones(condition.shape, bf16), jnp.zeros(condition.shape, bf16))
+
+
 def sender_kernel(views, tiles, copies, direct, centers, scale, angle, opacity, color, rank, dest, out, feat):
     rows = centers.shape[3]
     cap = 2 * rows // tiles
@@ -47,19 +51,23 @@
     cosine = jnp.cos(theta)
     sine = jnp.sin(theta)
     feat[...] = jnp.zeros_like(feat)
-    before = lax.broadcasted_iota(jnp.int32, (rows, rows), 0) < lax.broadcasted_iota(jnp.int32, (rows, rows), 1)
-    before = jnp.where(before, 1.0, 0.0).astype(bf16)
+    def count_up(shape, axis):
+        return lax.broadcasted_iota(jnp.int32, shape, axis).astype(f32).astype(bf16)
+
+    before = mark(count_up((rows, rows), 0) < count_up((rows, rows), 1))
     tile_id = lax.broadcasted_iota(jnp.int32, (hot_rows, rows), 0)
-    slot_id = lax.broadcasted_iota(jnp.int32, (slots, rows), 0)
+    slot_id = count_up((cap, rows), 0)
+    hot = [jnp.where(tile_id == dest[0, v], 1.0, 0.0) for v in range(views)]
+    hot = jnp.concatenate(hot, axis=0)
+    earlier = hot * jnp.dot(hot.astype(bf16), before, preferred_element_type=f32)
     for v in range(views):
+        feat[v, 0:2] = centers[0, v]
         s1 = scale[0, v, 0:1]
         s2 = scale[0, v, 1:2]
         i1 = 1.0 / (s1 * s1)
         i2 = 1.0 / (s2 * s2)
         c = cosine[v : v + 1]
         s = sine[v : v + 1]
-        feat[v, 0:1] = centers[0, v, 0:1]
-        feat[v, 1:2] = centers[0, v, 1:2]
         feat[v, 2:3] = c * c * i1 + s * s * i2
         feat[v, 3:4] = c * s * (i1 - i2)
         feat[v, 4:5] = s * s * i1 + c * c * i2
@@ -67,13 +75,11 @@
         for i in range(3):
             feat[v, 6 + i : 7 + i] = color[i]
         feat[v, 9:10] = rank[0, v : v + 1].astype(f32)
-
-        target = dest[0, v]
-        hot = jnp.where(tile_id == target, 1.0, 0.0)
-        earlier = jnp.dot(hot.astype(bf16), before, preferred_element_type=f32)
-        place = jnp.sum(hot * earlier, axis=0, keepdims=True).astype(jnp.int32)
-        slot = target * cap + place
-        pick = jnp.where(slot_id == slot, 1.0, 0.0).astype(bf16)
+    for v in range(views):
+        place = jnp.sum(earlier[v * hot_rows : (v + 1) * hot_rows], axis=0, keepdims=True)
+        slot = dest[0, v].astype(f32) * cap + place
+        pick = [mark(jnp.broadcast_to((slot - t * cap).astype(bf16), (cap, rows)) == slot_id) for t in range(tiles)]
+        pick = jnp.concatenate(pick, axis=0)
         stack = jnp.concatenate(pieces(feat[v], 3), axis=0)
         moved = lax.dot_general(stack, pick, NT, preferred_element_type=f32)
         moved = moved[0:16] + moved[16:32] + moved[32:48]
@@ -84,10 +90,6 @@
                     out[pl.ds(((v * copies + q) * tiles + t) * NF, NF), :] = block
         else:
             out[v] = moved[0:NF]
-
-
-def mark(condition):
-    return jnp.where(condition, jnp.ones(condition.shape, bf16), jnp.zeros(condition.shape, bf16))
 
 
 def positions(rank, real, slabs, n_ranks):

time: 21.1 us -> 20.7 us (0.981)
  the two profiles are of different devices: /device:TPU:1 before, /device:TPU:0 now
where the time goes in v6:
time: 20.7 us; the launch traced here: 20.9 us
  blocking collectives  15.8 us (76%)
  Pallas kernels  5.14 us (25%)
    all_to_all x1, blocking collectives, body(): lax.all_to_all(sent, ('slab', 'tile'), split_axis=0, concat_axis=0, tiled...  15.8 us
    pallas_call x1, Pallas kernels, body(): pl.pallas_call(partial(receiver_kernel, slabs, tiles, views, direct, tile...  3.91 us
    pallas_call x1, Pallas kernels, body(): pl.pallas_call(partial(sender_kernel, views, tiles, copies, direct), out_...  1.23 us

profile of v6, /device:TPU:0, one launch (start us, length us, event | category | flops | bytes accessed | tf_op | source)
XLA Modules:
  0.0 20.9 jit_solution(13697415739692425838)
XLA Ops:
  0.0 1.2 %sender.1 = f32[320,128]{1,0:T(8,128)S(1)} custom-call(f32[1,2,2,256]{3,2,1,0:T(2,128)} %centers.1, f32[1,2,2,256]{3,2,1,0:T(2,128)} %scale.1, f32[1,2,256]{2,1,0:T(2,128)} %angle.1, f32[1,256]{1,0:T(1,128)} %opacity.1, f32[3,1,256]{2,1,0:T(1,128)} %bitcast.6, s32[1,2,256]{2,1,0:T(2,128)} %rank.1, s32[1,2,1,256]{3,2,1,0:T(1,128)} %bitcast.7), custom_call_target="tpu_custom_call" | custom-call | tf_op jit(solution)/shard_map/sender/pallas_call | solution.py:323
  1.2 15.8 %all_to_all.5 = f32[32,1,1280]{2,1,0:T(1,128)S(1)} all-to-all(f32[32,1,1280]{2,1,0:T(1,128)S(1)} %bitcast.5), channel_id=1, replica_groups=mesh['slab'=8,'tile'=4] {'slab','tile'}, dimensions={0} | all-to-all | bytes 327680 | tf_op jit(solution)/shard_map/all_to_all | solution.py:335
  17.0 3.9 %receiver.1 = f32[4,1,512]{2,1,0:T(1,128)} custom-call(s32[2,8]{1,0:T(2,128)} %order_hbm.1, f32[320,128]{1,0:T(8,128)S(1)} %bitcast.4), custom_call_target="tpu_custom_call" | custom-call | tf_op jit(solution)/shard_map/receiver/pallas_call | solution.py:341
